TPU v7x, 256 devices: a whole 4x4x8 slice. The times are simulated.
256 devices in a mesh: dp: 32 (over y, z_lo, core), seq: 8 (over z_hi, x).
Axes of the slice: x: 4, y: 4, z: 8 (z_hi: 2, z_lo: 4; z = z_hi * 4 + z_lo), core: 2. Of those that a mesh axis runs over, the one named last changes fastest.
Arguments:
- stream_in: bfloat16 [32, 1024, 768], P('dp', 'seq'), may hold values from -30 to 30
- queries: bfloat16 [32, 1024, 768], P('dp', 'seq'), may hold values from -5.6 to 5.6
- key_rows: bfloat16 [32, 1024, 768], P('dp', 'seq'), may hold values from -5.6 to 5.6
- value_rows: bfloat16 [32, 1024, 768], P('dp', 'seq'), may hold values from -6 to 6
- conv_weight: bfloat16 [768, 5, 768], P('dp'), may hold values from -0.09375 to 0.09375
- cotangent: bfloat16 [32, 1024, 768], P('dp', 'seq'), may hold values from -6 to 6
Outputs:
- grad_stream: bfloat16 [32, 1024, 768], P('dp', 'seq')
- grad_queries: bfloat16 [32, 1024, 768], P('dp', 'seq')
- grad_keys: bfloat16 [32, 1024, 768], P('dp', 'seq')
- grad_values: bfloat16 [32, 1024, 768], P('dp', 'seq')
- grad_weight: float32 [768, 5, 768], P('dp')
All inputs are finite; a program needn't handle non-finite values.
Results may differ from a plain program's by a relative error of at most 0.017.
Values may be sent and summed in bfloat16 or wider, within the bound.
A program may use at most 128 MiB of HBM per device.

v0:
```python
import jax
import jax.numpy as jnp
from jax import lax
from jax.sharding import PartitionSpec as P

HEADS = 8
HEAD_DIM = 96
TAPS = 5


def padded(block, sides, width):
    for axis, dim in sides:
        count = lax.axis_size(axis)
        forward = [(i, i + 1) for i in range(count - 1)]
        backward = [(target, source) for source, target in forward]
        low = lax.ppermute(
            lax.slice_in_dim(block, block.shape[dim] - width, None, axis=dim), axis, forward
        )
        high = lax.ppermute(lax.slice_in_dim(block, 0, width, axis=dim), axis, backward)
        block = jnp.concatenate([low, block, high], axis=dim)
    return block


def activate(stream):
    square = jnp.mean(stream * stream, axis=-1, keepdims=True)
    return jax.nn.gelu(stream * lax.rsqrt(square + 1e-06), approximate=True)


def attend_forward(query, keys, values, scale):
    scores = jnp.einsum("rhd,nhd->hrn", query, keys, preferred_element_type=jnp.float32) * scale
    top = jnp.max(scores, axis=-1, keepdims=True)
    expo = jnp.exp(scores - top)
    total = jnp.sum(expo, axis=-1, keepdims=True)
    expo_b = expo.astype(jnp.bfloat16)
    attended = jnp.einsum("hrn,nhd->rhd", expo_b, values, preferred_element_type=jnp.float32)
    attended = attended / jnp.transpose(total, (1, 0, 2))
    return (expo, total, attended)


def attend_back(keys, values, expo, total, attended, dout, scale):
    probs = expo / total
    probs_b = probs.astype(jnp.bfloat16)
    delta = jnp.transpose(jnp.sum(dout.astype(jnp.float32) * attended, axis=-1), (1, 0))[:, :, None]
    dprob = jnp.einsum("rhd,nhd->hrn", dout, values, preferred_element_type=jnp.float32)
    dscore = (probs * (dprob - delta)).astype(jnp.bfloat16)
    grad_query = (
        jnp.einsum("hrn,nhd->rhd", dscore, keys, preferred_element_type=jnp.float32) * scale
    )
    return (dscore, probs_b, grad_query)


def body(stream_in, queries, key_rows, value_rows, conv_weight, cotangent):
    rows = queries.shape[1]
    channels = queries.shape[2]
    dp_count = lax.axis_size("dp")
    seq_count = lax.axis_size("seq")
    length = rows * seq_count
    scale = HEAD_DIM ** (-0.5)
    half = TAPS // 2
    query_local = queries[0].reshape(rows, HEADS, HEAD_DIM)
    keys_all, values_all = (
        lax.all_gather(key_rows, "seq", axis=1, tiled=True),
        lax.all_gather(value_rows, "seq", axis=1, tiled=True),
    )
    keys_full = keys_all[0].reshape(length, HEADS, HEAD_DIM)
    values_full = values_all[0].reshape(length, HEADS, HEAD_DIM)
    expo, total, attended = attend_forward(query_local, keys_full, values_full, scale)
    attended_flat = attended.reshape(rows, channels)
    stream = (stream_in[0].astype(jnp.float32) + attended_flat).astype(jnp.bfloat16)
    hidden, pullback = jax.vjp(activate, stream.astype(jnp.float32))
    hidden_b = hidden.astype(jnp.bfloat16)
    full_weight = lax.all_gather(conv_weight, "dp", axis=0, tiled=True)
    extended = padded(jnp.stack([hidden_b, cotangent[0]]), (("seq", 1),), half)
    hid_ext = extended[0]
    cot_ext = extended[1]
    cot_local = cotangent[0]
    windows = jnp.stack([hid_ext[tap : tap + rows] for tap in range(TAPS)], axis=1).reshape(
        rows, TAPS * channels
    )
    norm_factor = 1.0 / jnp.sqrt(jnp.float32(dp_count * length))
    owned = lax.psum_scatter(
        jnp.einsum("to,tk->ok", cot_local, windows, preferred_element_type=jnp.float32),
        "dp",
        scatter_dimension=0,
        tiled=True,
    )
    summed = lax.psum(owned, "seq")
    grad_weight = (summed * norm_factor).reshape(summed.shape[0], TAPS, channels)
    back = jnp.zeros((rows, channels), jnp.float32)
    for tap in range(TAPS):
        start = 2 * half - tap
        back = back + jnp.dot(
            cot_ext[start : start + rows],
            full_weight[:, tap, :],
            preferred_element_type=jnp.float32,
        )
    grad_stream = (cot_local.astype(jnp.float32) + pullback(back)[0]).astype(jnp.bfloat16)
    dout = grad_stream.reshape(rows, HEADS, HEAD_DIM)
    dscore, probs_b, grad_query = attend_back(
        keys_full, values_full, expo, total, attended, dout, scale
    )
    key_part = (
        jnp.einsum("hrn,rhd->nhd", dscore, query_local, preferred_element_type=jnp.float32) * scale
    )
    value_part = jnp.einsum("hrn,rhd->nhd", probs_b, dout, preferred_element_type=jnp.float32)
    key_sum, value_sum = (
        lax.psum_scatter(
            key_part.reshape(1, length, channels).astype(jnp.bfloat16),
            "seq",
            scatter_dimension=1,
            tiled=True,
        ).astype(jnp.float32),
        lax.psum_scatter(
            value_part.reshape(1, length, channels).astype(jnp.bfloat16),
            "seq",
            scatter_dimension=1,
            tiled=True,
        ).astype(jnp.float32),
    )
    grad_queries = grad_query.reshape(1, rows, channels).astype(jnp.bfloat16)
    grad_keys = key_sum.astype(jnp.bfloat16)
    grad_values = value_sum.astype(jnp.bfloat16)
    return (grad_stream[None], grad_queries, grad_keys, grad_values, grad_weight)


def solution(mesh):
    in_specs = (
        P("dp", "seq", None),
        P("dp", "seq", None),
        P("dp", "seq", None),
        P("dp", "seq", None),
        P("dp", None, None),
        P("dp", "seq", None),
    )
    out_specs = (
        P("dp", "seq", None),
        P("dp", "seq", None),
        P("dp", "seq", None),
        P("dp", "seq", None),
        P("dp", None, None),
    )
    return jax.shard_map(body, mesh=mesh, in_specs=in_specs, out_specs=out_specs, check_vma=False)
```

profile of v0, /device:TPU:8, one launch (start us, length us, event | category | flops | bytes accessed | tf_op | source)
XLA Modules:
  0.0 708.1 jit_solution(6786424331102835818)
XLA Ops:
  7.2 0.7 all-gather.4.cloned.1.call-update
  7.9 0.7 all-gather.6.cloned.1.call-update
  8.7 0.7 all-gather.8.cloned.1.call-update
  9.4 1.1 copy.35
  10.5 1.1 copy.39
  11.7 71.0 %all-gather.4.cloned.1.call-done = bf16[1,1024,768]{2,1,0:T(8,128)(2,1)} async-done(((bf16[1,128,768]{2,1,0:T(8,128)(2,1)}), bf16[1,1024,768]{2,1,0:T(8,128)(2,1)}) %all-gather.4.cloned.1.call-update) | async-done | bytes 1572880 | tf_op jit(solution)/shard_map/all_gather | solution.py:62
  82.7 1.7 copy.36
  84.4 65.9 %all-gather.6.cloned.1.call-done = bf16[1,1024,768]{2,1,0:T(8,128)(2,1)} async-done(((bf16[1,128,768]{2,1,0:T(8,128)(2,1)}), bf16[1,1024,768]{2,1,0:T(8,128)(2,1)}) %all-gather.6.cloned.1.call-update) | async-done | bytes 1572880 | tf_op jit(solution)/shard_map/all_gather | solution.py:63
  150.2 2.6 copy.37
  152.8 0.8 multiply_reduce_fusion
  153.7 0.9 fusion.1
  154.6 1.7 copy-done.10
  156.2 1.0 multiply_reduce_fusion.2
  157.4 0.2 fusion.35
  157.7 3.0 collective-permute-start.1
  160.8 1.3 collective-permute-start
  162.1 4.2 collective-permute-done
  166.4 0.7 fusion.48
  167.1 0.7 fusion.47
  167.9 0.7 bitcast_dynamic-update-slice_fusion
  168.6 0.7 fusion.46
  169.3 0.7 fusion.45
  170.0 1.6 copy.44
  171.6 6.0 convolution_bitcast_fusion
  177.6 12.5 %copy.47 = f32[768,3840]{1,0:T(8,128)} copy(f32[768,3840]{0,1:T(8,128)} %convolution_bitcast_fusion) | data formatting | bytes 23592960
  190.4 23.2 %all-gather.8.cloned.1.call-done = bf16[768,5,768]{2,0,1:T(8,128)(2,1)} async-done(((bf16[24,5,768]{2,0,1:T(8,128)(2,1)}), bf16[768,5,768]{2,0,1:T(8,128)(2,1)}) %all-gather.8.cloned.1.call-update) | async-done | bytes 5898256 | tf_op jit(solution)/shard_map/all_gather | solution.py:72
  213.6 1.6 fusion.15
  215.2 1.6 convolution_add_fusion.3
  216.8 1.6 convolution_add_fusion.2
  218.4 1.6 convolution_add_fusion.1
  220.1 1.9 fusion.41
  222.3 145.9 %reduce-scatter.10.cloned.1.call-done = f32[24,3840]{1,0:T(8,128)} async-done(((f32[768,3840]{1,0:T(8,128)}), f32[24,3840]{1,0:T(8,128)}) %reduce-scatter.10.cloned.1.call-update) | async-done | bytes 368656
  368.3 2.8 copy.48
  371.2 4.6 fusion.9
  375.8 2.7 copy.43
  378.5 0.2 reduce-scatter.6.cloned.1.call-start
  378.7 1.0 multiply_reduce_fusion.1
  379.7 3.9 multiply_convert_fusion
  383.7 1.3 copy-done.1
  385.0 0.6 multiply_convert_fusion.1
  385.6 1.7 copy.42
  387.3 2.4 fusion.16
  389.7 0.8 copy.45
  390.5 124.3 %all-reduce.2.cloned.1.call-done = f32[24,3840]{0,1:T(8,128)} async-done(((f32[24,3840]{0,1:T(8,128)}), f32[24,3840]{0,1:T(8,128)}) %all-reduce.2.cloned.1.call-update) | async-done | bytes 368656 | tf_op jit(solution)/shard_map/psum | solution.py:87
  514.8 1.7 broadcast_multiply_fusion
  516.5 1.3 copy.46
  517.8 92.6 %reduce-scatter.8.cloned.1.call-done = bf16[1,128,768]{2,1,0:T(8,128)(2,1)} async-done(((bf16[1,1024,768]{2,1,0:T(8,128)(2,1)}), bf16[1,128,768]{2,1,0:T(8,128)(2,1)}) %reduce-scatter.8.cloned.1.call-update) | async-done | bytes 196624 | tf_op jit(solution)/shard_map/reduce_scatter | solution.py:113
  610.4 90.9 %reduce-scatter.6.cloned.1.call-done = bf16[1,128,768]{2,1,0:T(8,128)(2,1)} async-done(((bf16[1,1024,768]{2,1,0:T(8,128)(2,1)}), bf16[1,128,768]{2,1,0:T(8,128)(2,1)}) %reduce-scatter.6.cloned.1.call-update) | async-done | bytes 196624 | tf_op jit(solution)/shard_map/reduce_scatter | solution.py:107
  (46 shorter events, 1.2 us)
Async XLA Ops:
  7.2 75.5 %all-gather.4.cloned.1.call-start = ((), (), s32[]{:S(2)}) async-start(), calls=%async_computation.3 | async-start | bytes 1769472 | tf_op jit(solution)/shard_map/all_gather | solution.py:62
  7.9 142.3 %all-gather.6.cloned.1.call-start = ((), (), s32[]{:S(2)}) async-start(), calls=%async_computation.4 | async-start | bytes 1769472 | tf_op jit(solution)/shard_map/all_gather | solution.py:63
  8.6 205.0 %all-gather.8.cloned.1.call-start = ((), (), s32[]{:S(2)}) async-start(), calls=%async_computation.5 | async-start | bytes 6082560 | tf_op jit(solution)/shard_map/all_gather | solution.py:72
  9.4 358.9 %reduce-scatter.10.cloned.1.call-start = ((), (), s32[]{:S(2)}) async-start(), calls=%async_computation.9 | async-start | bytes 12165120
  10.5 142.3 %copy-start.7 = (bf16[1,128,768]{1,2,0:T(8,128)(2,1)}, bf16[1,128,768]{1,2,0:T(8,128)(2,1)S(1)}, u32[]{:S(2)}) copy-start(bf16[1,128,768]{1,2,0:T(8,128)(2,1)S(1)} %copy.35) | copy-start | bytes 589828
  153.7 3.6 copy-start
  153.7 2.6 copy-start.10
  156.2 1.2 copy-start.9
  156.2 1.4 copy-start.2
  157.7 4.4 collective-permute-start.1
  160.8 5.5 collective-permute-start
  166.4 2.9 copy-start.3
  166.4 2.9 copy-start.5
  190.1 23.5 %copy-start.6 = (bf16[2,130,768]{2,1,0:T(8,128)(2,1)S(1)}, bf16[2,130,768]{2,1,0:T(8,128)(2,1)}, u32[]{:S(2)}) copy-start(bf16[2,130,768]{2,1,0:T(8,128)(2,1)} %copy-done.5) | copy-start | bytes 1198084
  190.2 324.6 %all-reduce.2.cloned.1.call-start = ((), (), s32[]{:S(2)}) async-start(), calls=%async_computation.8 | async-start | bytes 3932160 | tf_op jit(solution)/shard_map/psum | solution.py:87
  190.4 28.0 %copy-start.4 = (bf16[2,130,768]{2,1,0:T(8,128)(2,1)S(1)}, bf16[2,130,768]{2,1,0:T(8,128)(2,1)}, u32[]{:S(2)}) copy-start(bf16[2,130,768]{2,1,0:T(8,128)(2,1)} %copy-done.3) | copy-start | bytes 1198084
  222.2 149.0 %copy-start.12 = (bf16[128,768]{1,0:T(8,128)(2,1)}, bf16[128,768]{1,0:T(8,128)(2,1)S(1)}, u32[]{:S(2)}) copy-start(bf16[128,768]{1,0:T(8,128)(2,1)S(1)} %fusion.43) | copy-start | bytes 589828
  222.3 148.8 %copy-start.13 = (bf16[128,768]{0,1:T(8,128)(2,1)}, bf16[128,768]{0,1:T(8,128)(2,1)S(1)}, u32[]{:S(2)}) copy-start(bf16[128,768]{0,1:T(8,128)(2,1)S(1)} %copy.41) | copy-start | bytes 589828
  371.1 239.3 %reduce-scatter.8.cloned.1.call-start = ((), (), s32[]{:S(2)}) async-start(), calls=%async_computation.7 | async-start | bytes 1769472 | tf_op jit(solution)/shard_map/reduce_scatter | solution.py:113
  375.8 3.9 copy-start.11
  378.5 322.8 %reduce-scatter.6.cloned.1.call-start = ((), (), s32[]{:S(2)}) async-start(), calls=%async_computation.6 | async-start | bytes 1769472 | tf_op jit(solution)/shard_map/reduce_scatter | solution.py:107
  379.7 5.3 copy-start.8
  383.7 1.3 copy-start.1
Sparse Core Ops, SparseCore 0:
  10.6 72.0 all-gather.3
  85.3 64.9 all-gather.5
  152.0 61.5 all-gather.7
  216.1 152.1 reduce-scatter.9
  371.2 143.4 all-reduce.1
  519.2 91.0 reduce-scatter.7
  615.0 86.2 reduce-scatter.5
where the time goes:
time: 709 us; the launch traced here: 708 us
  waiting for transfers between devices  620 us (87%)
  local copies, waits for them, and re-layouts  37.1 us (5%)
  matrix products  27.6 us (4%)
  between operations  14.4 us (2%)
    unnamed x8, waiting for transfers between devices  148 us
    psum x1, waiting for transfers between devices, body(): summed = lax.psum(owned, 'seq')  124 us
    reduce_scatter x1, waiting for transfers between devices, body(): lax.psum_scatter(value_part.reshape(1, length, channels).astype(jnp.bfloa...  92.6 us
    reduce_scatter x1, waiting for transfers between devices, body(): lax.psum_scatter(key_part.reshape(1, length, channels).astype(jnp.bfloat1...  90.9 us
    all_gather x1, waiting for transfers between devices, body(): lax.all_gather(key_rows, 'seq', axis=1, tiled=True)  71 us
    all_gather x1, waiting for transfers between devices, body(): lax.all_gather(value_rows, 'seq', axis=1, tiled=True)  65.9 us
    unnamed x37, local copies, waits for them, and re-layouts  24.5 us
    all_gather x1, waiting for transfers between devices, body(): full_weight = lax.all_gather(conv_weight, 'dp', axis=0, tiled=True)  23.2 us
  transfers between devices with their start and end apart: 9, of which 8 were waited for; matrix products, arithmetic and copies ran while one was open for 9% of the time, Pallas kernels for 0%

commit v1 on v0

--- a/solution.py
+++ b/solution.py
@@ -6,6 +6,11 @@
 HEADS = 8
 HEAD_DIM = 96
 TAPS = 5
+
+
+def exchange_gather(shard, axis, d):
+    outgoing = jnp.stack([shard] * lax.axis_size(axis))
+    return jnp.concatenate(lax.all_to_all(outgoing, axis, 0, 0), axis=d)
 
 
 def padded(block, sides, width):
@@ -60,7 +65,7 @@
     query_local = queries[0].reshape(rows, HEADS, HEAD_DIM)
     keys_all, values_all = (
         lax.all_gather(key_rows, "seq", axis=1, tiled=True),
-        lax.all_gather(value_rows, "seq", axis=1, tiled=True),
+        exchange_gather(value_rows, "seq", 1),
     )
     keys_full = keys_all[0].reshape(length, HEADS, HEAD_DIM)
     values_full = values_all[0].reshape(length, HEADS, HEAD_DIM)

time: 709 us -> 660 us (0.931)
  waiting for transfers between devices: 620 us -> 558 us
  starting transfers between devices: 4.79 us -> 15.7 us
    all_gather x1 -> x0, waiting for transfers between devices: 65.9 us -> none  [body(): lax.all_gather(value_rows, 'seq', axis=1, tiled=True)]
    all_to_all x0 -> x1, waiting for transfers between devices: none -> 32.7 us  [exchange_gather(): return jnp.concatenate(lax.all_to_all(outgoing, axis, 0, 0), axis=d)]
    all_gather x1, waiting for transfers between devices: 71 us -> 42 us  [body(): lax.all_gather(key_rows, 'seq', axis=1, tiled=True)]
    all_to_all x0 -> x1, starting transfers between devices: none -> 10.9 us  [exchange_gather(): return jnp.concatenate(lax.all_to_all(outgoing, axis, 0, 0), axis=d)]
    unnamed x37 -> x43, local copies, waits for them, and re-layouts: 24.5 us -> 23.8 us
    unnamed x8 -> x7, waiting for transfers between devices: 148 us -> 148 us
  transfers between devices with their start and end apart: 9 -> 9, of which waited for: 8 -> 8; matrix products, arithmetic and copies ran while one was open for 9% -> 10% of each run, Pallas kernels for 0% -> 0%
where the time goes in v1:
time: 660 us; the launch traced here: 659 us
  waiting for transfers between devices  558 us (85%)
  local copies, waits for them, and re-layouts  39.1 us (6%)
  matrix products  27.6 us (4%)
  starting transfers between devices  15.7 us (2%)
  between operations  14.5 us (2%)
    unnamed x7, waiting for transfers between devices  148 us
    psum x1, waiting for transfers between devices, body(): summed = lax.psum(owned, 'seq')  125 us
    reduce_scatter x1, waiting for transfers between devices, body(): lax.psum_scatter(value_part.reshape(1, length, channels).astype(jnp.bfloa...  92.6 us
    reduce_scatter x1, waiting for transfers between devices, body(): lax.psum_scatter(key_part.reshape(1, length, channels).astype(jnp.bfloat1...  90.7 us
    all_gather x1, waiting for transfers between devices, body(): lax.all_gather(key_rows, 'seq', axis=1, tiled=True)  42 us
    all_to_all x1, waiting for transfers between devices, exchange_gather(): return jnp.concatenate(lax.all_to_all(outgoing, axis, 0, 0), axis=d)  32.7 us
    all_gather x1, waiting for transfers between devices, body(): full_weight = lax.all_gather(conv_weight, 'dp', axis=0, tiled=True)  23.9 us
    unnamed x43, local copies, waits for them, and re-layouts  23.8 us
  transfers between devices with their start and end apart: 9, of which 8 were waited for; matrix products, arithmetic and copies ran while one was open for 10% of the time, Pallas kernels for 0%

profile of v1, /device:TPU:8, one launch (start us, length us, event | category | flops | bytes accessed | tf_op | source)
XLA Modules:
  0.0 659.4 jit_solution(12837300147549064163)
XLA Ops:
  7.2 0.7 all-gather.3.cloned.1.call-update
  8.0 0.7 all-gather.5.cloned.1.call-update
  8.7 1.1 copy.37
  9.8 1.4 stack.16
  11.1 10.9 %all-to-all-start = ((bf16[8,1,128,768]{2,3,1,0:T(8,128)(2,1)}), bf16[8,1,128,768]{2,3,1,0:T(8,128)(2,1)S(1)}, u32[]{:S(2)}, u32[]{:S(2)}) async-start(bf16[8,1,128,768]{2,3,1,0:T(8,128)(2,1)} %stack.16), calls=%async_computation | async-start | bytes 3145728 | tf_op jit(solution)/shard_map/all_to_all | solution.py:13
  22.3 0.9 copy.40
  23.2 32.7 %all-to-all-done = bf16[8,1,128,768]{2,3,1,0:T(8,128)(2,1)S(1)} async-done(((bf16[8,1,128,768]{2,3,1,0:T(8,128)(2,1)}), bf16[8,1,128,768]{2,3,1,0:T(8,128)(2,1)S(1)}, u32[]{:S(2)}, u32[]{:S(2)}) %all-to-all-start) | async-done | bytes 1572896 | tf_op jit(solution)/shard_map/all_to_all | solution.py:13
  55.9 1.0 copy.38
  57.0 2.1 reshape_squeeze_reshape.3
  59.0 42.0 %all-gather.3.cloned.1.call-done = bf16[1,1024,768]{2,1,0:T(8,128)(2,1)} async-done(((bf16[1,128,768]{2,1,0:T(8,128)(2,1)}), bf16[1,1024,768]{2,1,0:T(8,128)(2,1)}) %all-gather.3.cloned.1.call-update) | async-done | bytes 1572880 | tf_op jit(solution)/shard_map/all_gather | solution.py:67
  101.0 1.7 copy.36
  102.8 0.8 multiply_reduce_fusion
  103.6 0.9 fusion.1
  104.5 1.7 copy-done.11
  106.5 1.0 multiply_reduce_fusion.2
  108.0 3.0 collective-permute-start.1
  111.0 1.3 collective-permute-start
  112.4 4.2 collective-permute-done
  116.7 0.7 fusion.48
  117.4 0.7 fusion.47
  118.2 0.7 bitcast_dynamic-update-slice_fusion
  118.8 0.7 fusion.46
  119.6 0.7 fusion.45
  120.3 1.6 copy.45
  121.9 6.0 convolution_bitcast_fusion
  127.9 12.5 %copy.48 = f32[768,3840]{1,0:T(8,128)} copy(f32[768,3840]{0,1:T(8,128)} %convolution_bitcast_fusion) | data formatting | bytes 23592960
  140.7 23.9 %all-gather.5.cloned.1.call-done = bf16[768,5,768]{2,0,1:T(8,128)(2,1)} async-done(((bf16[24,5,768]{2,0,1:T(8,128)(2,1)}), bf16[768,5,768]{2,0,1:T(8,128)(2,1)}) %all-gather.5.cloned.1.call-update) | async-done | bytes 5898256 | tf_op jit(solution)/shard_map/all_gather | solution.py:77
  164.6 1.6 fusion.15
  166.2 1.6 convolution_add_fusion.3
  167.8 1.6 convolution_add_fusion.2
  169.4 1.6 convolution_add_fusion.1
  171.0 1.9 fusion.41
  173.3 146.1 %reduce-scatter.10.cloned.1.call-done = f32[24,3840]{1,0:T(8,128)} async-done(((f32[768,3840]{1,0:T(8,128)}), f32[24,3840]{1,0:T(8,128)}) %reduce-scatter.10.cloned.1.call-update) | async-done | bytes 368656
  319.4 2.8 copy.49
  322.5 4.6 fusion.9
  327.1 2.7 copy.44
  329.9 1.0 multiply_reduce_fusion.1
  330.9 3.9 multiply_convert_fusion
  334.8 1.3 copy-done.1
  336.2 0.6 multiply_convert_fusion.1
  336.7 1.7 copy.43
  338.4 2.4 fusion.16
  340.8 0.8 copy.46
  341.6 124.6 %all-reduce.2.cloned.1.call-done = f32[24,3840]{0,1:T(8,128)} async-done(((f32[24,3840]{0,1:T(8,128)}), f32[24,3840]{0,1:T(8,128)}) %all-reduce.2.cloned.1.call-update) | async-done | bytes 368656 | tf_op jit(solution)/shard_map/psum | solution.py:92
  466.2 1.7 broadcast_multiply_fusion
  467.9 1.3 copy.47
  469.2 92.6 %reduce-scatter.8.cloned.1.call-done = bf16[1,128,768]{2,1,0:T(8,128)(2,1)} async-done(((bf16[1,1024,768]{2,1,0:T(8,128)(2,1)}), bf16[1,128,768]{2,1,0:T(8,128)(2,1)}) %reduce-scatter.8.cloned.1.call-update) | async-done | bytes 196624 | tf_op jit(solution)/shard_map/reduce_scatter | solution.py:118
  561.8 90.7 %reduce-scatter.6.cloned.1.call-done = bf16[1,128,768]{2,1,0:T(8,128)(2,1)} async-done(((bf16[1,1024,768]{2,1,0:T(8,128)(2,1)}), bf16[1,128,768]{2,1,0:T(8,128)(2,1)}) %reduce-scatter.6.cloned.1.call-update) | async-done | bytes 196624 | tf_op jit(solution)/shard_map/reduce_scatter | solution.py:112
  (54 shorter events, 2.2 us)
Async XLA Ops:
  7.2 14.9 %copy-start.16 = (bf16[1,128,768]{2,1,0:T(8,128)(2,1)S(1)}, bf16[1,128,768]{2,1,0:T(8,128)(2,1)}, u32[]{:S(2)}) copy-start(bf16[1,128,768]{2,1,0:T(8,128)(2,1)} %param.7) | copy-start | bytes 589828
  7.2 15.1 %copy-start.9 = (bf16[1,128,768]{2,1,0:T(8,128)(2,1)S(1)}, bf16[1,128,768]{2,1,0:T(8,128)(2,1)}, u32[]{:S(2)}) copy-start(bf16[1,128,768]{2,1,0:T(8,128)(2,1)} %param.6) | copy-start | bytes 589828
  7.2 93.8 %all-gather.3.cloned.1.call-start = ((), (), s32[]{:S(2)}) async-start(), calls=%async_computation.4 | async-start | bytes 1769472 | tf_op jit(solution)/shard_map/all_gather | solution.py:67
  7.9 156.6 %all-gather.5.cloned.1.call-start = ((), (), s32[]{:S(2)}) async-start(), calls=%async_computation.5 | async-start | bytes 6082560 | tf_op jit(solution)/shard_map/all_gather | solution.py:77
  11.1 44.8 %all-to-all-start = ((bf16[8,1,128,768]{2,3,1,0:T(8,128)(2,1)}), bf16[8,1,128,768]{2,3,1,0:T(8,128)(2,1)S(1)}, u32[]{:S(2)}, u32[]{:S(2)}) async-start(bf16[8,1,128,768]{2,3,1,0:T(8,128)(2,1)} %stack.16), calls=%async_computation | async-start | bytes 3145728 | tf_op jit(solution)/shard_map/all_to_all | solution.py:13
  22.1 297.3 %reduce-scatter.10.cloned.1.call-start = ((), (), s32[]{:S(2)}) async-start(), calls=%async_computation.9 | async-start | bytes 12165120
  22.3 80.5 %copy-start.7 = (bf16[1,128,768]{1,2,0:T(8,128)(2,1)}, bf16[1,128,768]{1,2,0:T(8,128)(2,1)S(1)}, u32[]{:S(2)}) copy-start(bf16[1,128,768]{1,2,0:T(8,128)(2,1)S(1)} %copy.35) | copy-start | bytes 589828
  103.6 3.9 copy-start
  103.6 2.6 copy-start.11
  103.6 2.9 copy-start.15
  106.5 1.2 copy-start.10
  106.5 1.4 copy-start.2
  108.0 4.4 collective-permute-start.1
  111.0 5.5 collective-permute-start
  116.7 2.9 copy-start.3
  116.7 2.9 copy-start.5
  140.4 24.2 %copy-start.6 = (bf16[2,130,768]{2,1,0:T(8,128)(2,1)S(1)}, bf16[2,130,768]{2,1,0:T(8,128)(2,1)}, u32[]{:S(2)}) copy-start(bf16[2,130,768]{2,1,0:T(8,128)(2,1)} %copy-done.5) | copy-start | bytes 1198084
  140.4 325.8 %all-reduce.2.cloned.1.call-start = ((), (), s32[]{:S(2)}) async-start(), calls=%async_computation.8 | async-start | bytes 3932160 | tf_op jit(solution)/shard_map/psum | solution.py:92
  140.7 28.7 %copy-start.4 = (bf16[2,130,768]{2,1,0:T(8,128)(2,1)S(1)}, bf16[2,130,768]{2,1,0:T(8,128)(2,1)}, u32[]{:S(2)}) copy-start(bf16[2,130,768]{2,1,0:T(8,128)(2,1)} %copy-done.3) | copy-start | bytes 1198084
  173.1 149.4 %copy-start.13 = (bf16[128,768]{1,0:T(8,128)(2,1)}, bf16[128,768]{1,0:T(8,128)(2,1)S(1)}, u32[]{:S(2)}) copy-start(bf16[128,768]{1,0:T(8,128)(2,1)S(1)} %fusion.43) | copy-start | bytes 589828
  173.3 149.2 %copy-start.14 = (bf16[128,768]{0,1:T(8,128)(2,1)}, bf16[128,768]{0,1:T(8,128)(2,1)S(1)}, u32[]{:S(2)}) copy-start(bf16[128,768]{0,1:T(8,128)(2,1)S(1)} %copy.42) | copy-start | bytes 589828
  322.2 239.6 %reduce-scatter.8.cloned.1.call-start = ((), (), s32[]{:S(2)}) async-start(), calls=%async_computation.7 | async-start | bytes 1769472 | tf_op jit(solution)/shard_map/reduce_scatter | solution.py:118
  327.1 3.7 copy-start.12
  329.8 322.7 %reduce-scatter.6.cloned.1.call-start = ((), (), s32[]{:S(2)}) async-start(), calls=%async_computation.6 | async-start | bytes 1769472 | tf_op jit(solution)/shard_map/reduce_scatter | solution.py:112
  330.9 5.3 copy-start.8
  334.8 1.3 copy-start.1
Sparse Core Ops, SparseCore 0:
  10.6 90.3 all-gather.2
  102.8 61.6 all-gather.4
  167.1 152.2 reduce-scatter.9
  322.4 143.7 all-reduce.1
  470.7 91.1 reduce-scatter.7
  566.3 86.1 reduce-scatter.5
